TPU v7x, 32 devices: a whole 2x2x4 slice. The times are simulated.
32 devices in a mesh: fsdp: 4 (over y, x), ctx: 8 (over z, core).
Axes of the slice: x: 2, y: 2, z: 4, core: 2. Of those that a mesh axis runs over, the one named last changes fastest.
Arguments:
- tokens: bfloat16 [4, 1024, 5376], P('fsdp', 'ctx'), may hold values from -6 to 6
- pre_gain: float32 [5376], replicated, may hold values from 0.1 to 1.9
- w_query: bfloat16 [5376, 3072], P(None, 'fsdp'), may hold values from -0.078125 to 0.078125
- key_weight: bfloat16 [5376, 1536], P(None, 'fsdp'), may hold values from -0.078125 to 0.078125
- value_weight: bfloat16 [5376, 1536], P(None, 'fsdp'), may hold values from -0.078125 to 0.078125
- query_norm_gain: float32 [128], replicated, may hold values from 0.1 to 1.9
- key_gain: float32 [128], replicated, may hold values from 0.1 to 1.9
- w_out: bfloat16 [3072, 5376], P('fsdp'), may hold values from -0.109375 to 0.109375
- post_gain: float32 [5376], replicated, may hold values from 0.1 to 1.9
Outputs:
- layer_out: bfloat16 [4, 1024, 5376], P('fsdp', 'ctx')
All inputs are finite; a program needn't handle non-finite values.
Results may differ from a plain program's by a relative error of at most 0.012.
Values may be sent and summed in bfloat16 or wider, within the bound.
A program may use at most 128 MiB of HBM per device.

v0:
```python
import jax
import jax.numpy as jnp
from jax import lax
from jax.sharding import PartitionSpec as P

epsilon = 1e-06
score_scale = 168.0 ** (-0.5)


def passed_along(shard, axis, by):
    peers = lax.axis_size(axis)
    pairs = [(i, i + by) for i in range(peers) if 0 <= i + by < peers]
    return lax.ppermute(shard, axis, pairs)


def root_mean_norm(values, gain):
    mean_sq = jnp.mean(values * values, axis=-1, keepdims=True)
    return values * lax.rsqrt(mean_sq + epsilon) * gain


def rotary_embed(values, token_positions):
    half_dim = values.shape[-1] // 2
    frequencies = 10000.0 ** (-jnp.arange(half_dim, dtype=jnp.float32) / half_dim)
    angles = token_positions.astype(jnp.float32)[:, None] * frequencies[None, :]
    cosine = jnp.cos(angles)[:, None, :]
    sine_part = jnp.sin(angles)[:, None, :]
    first_half = values[..., :half_dim]
    second_half = values[..., half_dim:]
    return jnp.concatenate(
        [
            first_half * cosine - second_half * sine_part,
            second_half * cosine + first_half * sine_part,
        ],
        axis=-1,
    )


def per_device(
    tokens, pre_gain, w_query, key_weight, value_weight, query_norm_gain, key_gain, w_out, post_gain
):
    doc_rows, slab_rows, features = tokens.shape
    head_dim = query_norm_gain.shape[0]
    q_heads = w_query.shape[1] // head_dim
    kv_heads = key_weight.shape[1] // head_dim
    query_group_size = q_heads // kv_heads
    reach = 8 * slab_rows
    normalized_rows = root_mean_norm(tokens.astype(jnp.float32), pre_gain).astype(jnp.bfloat16)
    token_positions = lax.axis_index("ctx") * slab_rows + jnp.arange(slab_rows, dtype=jnp.int32)
    shard_rows = lax.all_gather(normalized_rows, "fsdp", axis=0, tiled=True)
    row_count = shard_rows.shape[0]
    flat_rows = shard_rows.reshape(row_count * slab_rows, features)
    query_rows = jnp.dot(flat_rows, w_query, preferred_element_type=jnp.float32).reshape(
        row_count, slab_rows, q_heads, head_dim
    )
    key_portion = jnp.dot(flat_rows, key_weight, preferred_element_type=jnp.float32).reshape(
        row_count, slab_rows, kv_heads, head_dim
    )
    value_portion = jnp.dot(flat_rows, value_weight, preferred_element_type=jnp.float32).reshape(
        row_count, slab_rows, kv_heads * head_dim
    )
    query_rows = rotary_embed(root_mean_norm(query_rows, query_norm_gain), token_positions).reshape(
        row_count, slab_rows, q_heads * head_dim
    )
    key_portion = rotary_embed(root_mean_norm(key_portion, key_gain), token_positions).reshape(
        row_count, slab_rows, kv_heads * head_dim
    )
    projected_all = jnp.concatenate([query_rows, key_portion, value_portion], axis=-1).astype(
        jnp.bfloat16
    )
    all_docs = projected_all.shape[0]
    query_rows = projected_all[..., : q_heads * head_dim].reshape(
        all_docs, slab_rows, kv_heads, query_group_size, head_dim
    )
    pairs = projected_all[..., q_heads * head_dim :]
    current = pairs
    pieces = [pairs]
    for rounds in range(8):
        current = passed_along(current, "ctx", 1)
        pieces = [current] + pieces
    windowed = jnp.concatenate(pieces, axis=1)
    key_count = windowed.shape[1]
    key_portion = windowed[..., : kv_heads * head_dim].reshape(
        all_docs, key_count, kv_heads, head_dim
    )
    value_portion = windowed[..., kv_heads * head_dim :].reshape(
        all_docs, key_count, kv_heads, head_dim
    )
    key_pos = token_positions[0] - reach + jnp.arange(key_count, dtype=jnp.int32)
    allowed = (
        (key_pos[None, :] >= 0)
        & (key_pos[None, :] <= token_positions[:, None])
        & (token_positions[:, None] - key_pos[None, :] < reach)
    )
    scores = (
        jnp.einsum("dqhgc,dkhc->dhgqk", query_rows, key_portion, preferred_element_type=jnp.float32)
        * score_scale
    )
    unnorm = jnp.where(allowed, jnp.exp(scores), 0.0)
    totals = jnp.sum(unnorm, axis=-1, keepdims=True)
    weights = (unnorm / totals).astype(jnp.bfloat16)
    attended = jnp.einsum(
        "dhgqk,dkhc->dqhgc", weights, value_portion, preferred_element_type=jnp.float32
    )
    attended = attended.astype(jnp.bfloat16).reshape(all_docs, slab_rows, q_heads * head_dim)
    row_count = doc_rows * lax.axis_size("fsdp")
    flat_rows = attended.reshape(row_count * slab_rows, q_heads * head_dim)
    summed = lax.psum_scatter(
        jnp.dot(flat_rows, w_out, preferred_element_type=jnp.float32)
        .reshape(row_count, slab_rows, features)
        .astype(jnp.bfloat16),
        "fsdp",
        scatter_dimension=0,
        tiled=True,
    ).astype(jnp.float32)
    return (tokens.astype(jnp.float32) + root_mean_norm(summed, post_gain)).astype(jnp.bfloat16)


def solution(mesh):
    return jax.shard_map(
        per_device,
        mesh=mesh,
        in_specs=(
            P("fsdp", "ctx", None),
            P(),
            P(None, "fsdp"),
            P(None, "fsdp"),
            P(None, "fsdp"),
            P(),
            P(),
            P("fsdp", None),
            P(),
        ),
        out_specs=P("fsdp", "ctx", None),
        check_vma=False,
    )
```

profile of v0, /device:TPU:25, one launch (start us, length us, event | category | flops | bytes accessed | tf_op | source)
XLA Modules:
  0.0 314.2 jit_solution(13279565401028772290)
XLA Ops:
  6.5 1.7 fusion.11
  8.2 2.8 fusion.13
  11.1 6.4 %copy.27 = bf16[5376,384]{0,1:T(8,128)(2,1)} copy(bf16[5376,384]{1,0:T(8,128)(2,1)} %param.12) | data formatting | bytes 8257536 | tf_op args[3]
  17.7 57.8 %all-gather.2.cloned.1.call-done = bf16[4,128,5376]{2,1,0:T(8,128)(2,1)} async-done(((bf16[1,128,5376]{2,1,0:T(8,128)(2,1)}), bf16[4,128,5376]{2,1,0:T(8,128)(2,1)}) %all-gather.2.cloned.1.call-update) | async-done | bytes 5505040 | tf_op jit(solution)/shard_map/all_gather | solution.py:49
  75.5 5.6 %multiply_reduce_fusion.1 = (f32[4,128,3]{1,2,0:T(4,128)S(1)}, f32[4,128,3,128]{1,3,2,0:T(8,128)S(1)}) fusion(bf16[3,128,5376,1]{2,1,0,3:T(8,128)(2,1)} %bitcast.64, bf16[4,128,5376]{2,1,0:T(8,128)(2,1)} %all-gather.2.cloned.1.call-done), kind=kOutput, calls=%fused_computation.32 | convolution fusion | flops 2114320896 | bytes 10426368 | tf_op jit(solution)/shard_map/dot_general | solution.py:55
  81.7 6.8 %fusion.16 = bf16[4,128,384]{2,1,0:T(8,128)(2,1)S(1)} fusion(bf16[4,128,5376]{2,1,0:T(8,128)(2,1)} %all-gather.2.cloned.1.call-done, bf16[5376,384]{1,0:T(8,128)(2,1)} %param.13), kind=kOutput, calls=%fused_computation.26 | convolution fusion | flops 2114125824 | bytes 10027008 | tf_op jit(solution)/shard_map/dot_general | solution.py:58
  89.9 3.2 %collective-permute-done = bf16[4,128,768]{2,1,0:T(8,128)(2,1)S(1)} collective-permute-done((bf16[4,128,768]{2,1,0:T(8,128)(2,1)S(1)}, bf16[4,128,768]{2,1,0:T(8,128)(2,1)S(1)}, u32[]{:S(2)}, u32[]{:S(2)}) %collective-permute-start) | collective-permute-done | bytes 786464 | tf_op jit(solution)/shard_map/ppermute | solution.py:13
  94.4 12.0 %collective-permute-done.1 = bf16[4,128,768]{2,1,0:T(8,128)(2,1)S(1)} collective-permute-done((bf16[4,128,768]{2,1,0:T(8,128)(2,1)S(1)}, bf16[4,128,768]{2,1,0:T(8,128)(2,1)S(1)}, u32[]{:S(2)}, u32[]{:S(2)}) %collective-permute-start.1) | collective-permute-done | bytes 786464 | tf_op jit(solution)/shard_map/ppermute | solution.py:13
  107.7 12.0 %collective-permute-done.2 = bf16[4,128,768]{2,1,0:T(8,128)(2,1)S(1)} collective-permute-done((bf16[4,128,768]{2,1,0:T(8,128)(2,1)S(1)}, bf16[4,128,768]{2,1,0:T(8,128)(2,1)S(1)}, u32[]{:S(2)}, u32[]{:S(2)}) %collective-permute-start.2) | collective-permute-done | bytes 786464 | tf_op jit(solution)/shard_map/ppermute | solution.py:13
  121.0 12.0 %collective-permute-done.3 = bf16[4,128,768]{2,1,0:T(8,128)(2,1)S(1)} collective-permute-done((bf16[4,128,768]{2,1,0:T(8,128)(2,1)S(1)}, bf16[4,128,768]{2,1,0:T(8,128)(2,1)S(1)}, u32[]{:S(2)}, u32[]{:S(2)}) %collective-permute-start.3) | collective-permute-done | bytes 786464 | tf_op jit(solution)/shard_map/ppermute | solution.py:13
  135.2 12.1 %collective-permute-done.4 = bf16[4,128,768]{2,1,0:T(8,128)(2,1)} collective-permute-done((bf16[4,128,768]{2,1,0:T(8,128)(2,1)S(1)}, bf16[4,128,768]{2,1,0:T(8,128)(2,1)}, u32[]{:S(2)}, u32[]{:S(2)}) %collective-permute-start.4) | collective-permute-done | bytes 786464 | tf_op jit(solution)/shard_map/ppermute | solution.py:13
  148.6 11.5 %copy.31 = bf16[5376,768]{0,1:T(8,128)(2,1)} copy(bf16[5376,768]{1,0:T(8,128)(2,1)} %param.11) | data formatting | bytes 16515072 | tf_op args[2]
  163.0 8.0 %multiply_reduce_fusion = (f32[4,128,6]{1,2,0:T(8,128)S(1)}, f32[4,128,6,128]{1,3,2,0:T(8,128)S(1)}) fusion(bf16[6,128,5376,1]{2,1,0,3:T(8,128)(2,1)} %bitcast.63, bf16[4,128,5376]{2,1,0:T(8,128)(2,1)} %all-gather.2.cloned.1.call-done), kind=kOutput, calls=%fused_computation.24 | convolution fusion | flops 4228641792 | bytes 15347712 | tf_op jit(solution)/shard_map/dot_general | solution.py:52
  171.0 4.8 %collective-permute-done.6 = bf16[4,128,768]{2,1,0:T(8,128)(2,1)S(1)} collective-permute-done((bf16[4,128,768]{2,1,0:T(8,128)(2,1)}, bf16[4,128,768]{2,1,0:T(8,128)(2,1)S(1)}, u32[]{:S(2)}, u32[]{:S(2)}) %collective-permute-start.6) | collective-permute-done | bytes 786464 | tf_op jit(solution)/shard_map/ppermute | solution.py:13
  178.8 10.3 %collective-permute-done.7 = bf16[4,128,768]{2,1,0:T(8,128)(2,1)S(1)} collective-permute-done((bf16[4,128,768]{2,1,0:T(8,128)(2,1)S(1)}, bf16[4,128,768]{2,1,0:T(8,128)(2,1)S(1)}, u32[]{:S(2)}, u32[]{:S(2)}) %collective-permute-start.7) | collective-permute-done | bytes 786464 | tf_op jit(solution)/shard_map/ppermute | solution.py:13
  191.9 2.5 fusion.23
  194.5 5.8 %copy.30 = bf16[4,1152,384]{1,2,0:T(8,128)(2,1)} copy(bf16[4,1152,384]{2,1,0:T(8,128)(2,1)} %get-tuple-element.5) | data formatting | bytes 7077888 | tf_op jit(solution)/shard_map/slice | solution.py:82
  200.3 4.0 %copy.29 = bf16[4,1152,384]{1,2,0:T(8,128)(2,1)} copy(bf16[4,1152,384]{2,1,0:T(8,128)(2,1)S(1)} %get-tuple-element.6) | data formatting | bytes 7077888 | tf_op jit(solution)/shard_map/slice | solution.py:85
  204.3 10.7 %fusion = (f32[4,3,2,128]{3,2,1,0:T(2,128)S(1)}, f32[4,3,1152,128,2]{3,2,4,1,0:T(8,128)}) fusion(pred[128,1152]{0,1:T(8,128)(4,1)} %fusion.19, bf16[4,1152,3,128,1]{1,3,4,2,0:T(8,128)(2,1)} %bitcast.66, bf16[4,128,3,2,128]{1,4,3,2,0:T(8,128)(2,1)} %bitcast.68), kind=kOutput, calls=%fused_computation.2 | convolution fusion | flops 916583424 | bytes 18640896 | tf_op jit(solution)/shard_map/dqhgc,dkhc->dhgqk/dot_general | solution.py:95
  215.0 8.7 %fusion.15 = bf16[4,3,128,2,128]{4,2,3,1,0:T(8,128)(2,1)S(1)} fusion(bf16[4,1152,3,128,1]{1,3,4,2,0:T(8,128)(2,1)S(1)} %bitcast.65, f32[4,3,1152,128,2]{3,2,4,1,0:T(8,128)} %get-tuple-element.18, f32[4,3,2,128]{3,2,1,0:T(2,128)S(1)} %get-tuple-element.17, pred[128,1152]{0,1:T(8,128)(4,1)S(1)} %copy-done.4), kind=kOutput, calls=%fused_computation.25 | convolution fusion | flops 920518656 | bytes 18640896 | tf_op jit(solution)/shard_map/dhgqk,dkhc->dqhgc/dot_general | solution.py:101
  223.7 6.5 %convolution_convert_fusion = bf16[4,128,5376]{2,1,0:T(8,128)(2,1)} fusion(bf16[4,128,768]{1,2,0:T(8,128)(2,1)S(1)} %bitcast.72, bf16[768,5376]{1,0:T(8,128)(2,1)S(1)} %bitcast.71), kind=kOutput, calls=%fused_computation.3 | convolution fusion | flops 4230610944 | bytes 14548992 | tf_op jit(solution)/shard_map/dot_general | solution.py:108
  230.3 72.4 %reduce-scatter.4.cloned.1.call-done = bf16[1,128,5376]{2,1,0:T(8,128)(2,1)} async-done(((bf16[4,128,5376]{2,1,0:T(8,128)(2,1)}), bf16[1,128,5376]{2,1,0:T(8,128)(2,1)}) %reduce-scatter.4.cloned.1.call-update) | async-done | bytes 1376272
  302.7 1.7 fusion.9
  304.4 3.0 fusion.14
  (61 shorter events, 18.0 us)
Async XLA Ops:
  6.5 69.0 %all-gather.2.cloned.1.call-start = ((), (), s32[]{:S(2)}) async-start(), calls=%async_computation.1 | async-start | bytes 6881280 | tf_op jit(solution)/shard_map/all_gather | solution.py:49
  11.1 291.6 %reduce-scatter.4.cloned.1.call-start = ((), (), s32[]{:S(2)}) async-start(), calls=%async_computation.2 | async-start | bytes 6881280
  75.5 5.7 %copy-start.6 = (f32[128]{0:T(128)S(1)}, f32[128]{0:T(128)}, u32[]{:S(2)}) copy-start(f32[128]{0:T(128)} %param.15) | copy-start | bytes 1540
  88.6 4.5 %collective-permute-start = (bf16[4,128,768]{2,1,0:T(8,128)(2,1)S(1)}, bf16[4,128,768]{2,1,0:T(8,128)(2,1)S(1)}, u32[]{:S(2)}, u32[]{:S(2)}) collective-permute-start(bf16[4,128,768]{2,1,0:T(8,128)(2,1)S(1)} %pad_maximum_fusion), channel_id=1, source_target_pairs={{0,1},{1,2},{2,3},{3,4},{4,5},{5,6},{6,7},{8,9},{9,10},{10,11},{11... | collective-permute-start | bytes 2359304 | tf_op jit(solution)/shard_map/ppermute | solution.py:13
  93.2 13.3 %collective-permute-start.1 = (bf16[4,128,768]{2,1,0:T(8,128)(2,1)S(1)}, bf16[4,128,768]{2,1,0:T(8,128)(2,1)S(1)}, u32[]{:S(2)}, u32[]{:S(2)}) collective-permute-start(bf16[4,128,768]{2,1,0:T(8,128)(2,1)S(1)} %collective-permute-done), channel_id=1, source_target_pairs={{0,1},{1,2},{2,3},{3,4},{4,5},{5,6},{6,7},{8,9},{9,10},{10,11},{11... | collective-permute-start | bytes 2359304 | tf_op jit(solution)/shard_map/ppermute | solution.py:13
  106.5 13.3 %collective-permute-start.2 = (bf16[4,128,768]{2,1,0:T(8,128)(2,1)S(1)}, bf16[4,128,768]{2,1,0:T(8,128)(2,1)S(1)}, u32[]{:S(2)}, u32[]{:S(2)}) collective-permute-start(bf16[4,128,768]{2,1,0:T(8,128)(2,1)S(1)} %collective-permute-done.1), channel_id=1, source_target_pairs={{0,1},{1,2},{2,3},{3,4},{4,5},{5,6},{6,7},{8,9},{9,10},{10,11},{11... | collective-permute-start | bytes 2359304 | tf_op jit(solution)/shard_map/ppermute | solution.py:13
  119.8 13.3 %collective-permute-start.3 = (bf16[4,128,768]{2,1,0:T(8,128)(2,1)S(1)}, bf16[4,128,768]{2,1,0:T(8,128)(2,1)S(1)}, u32[]{:S(2)}, u32[]{:S(2)}) collective-permute-start(bf16[4,128,768]{2,1,0:T(8,128)(2,1)S(1)} %collective-permute-done.2), channel_id=1, source_target_pairs={{0,1},{1,2},{2,3},{3,4},{4,5},{5,6},{6,7},{8,9},{9,10},{10,11},{11... | collective-permute-start | bytes 2359304 | tf_op jit(solution)/shard_map/ppermute | solution.py:13
  133.0 0.9 copy-start.2
  133.9 13.4 %collective-permute-start.4 = (bf16[4,128,768]{2,1,0:T(8,128)(2,1)S(1)}, bf16[4,128,768]{2,1,0:T(8,128)(2,1)}, u32[]{:S(2)}, u32[]{:S(2)}) collective-permute-start(bf16[4,128,768]{2,1,0:T(8,128)(2,1)S(1)} %collective-permute-done.3), channel_id=1, source_target_pairs={{0,1},{1,2},{2,3},{3,4},{4,5},{5,6},{6,7},{8,9},{9,10},{10,11},{11... | collective-permute-start | bytes 2359304 | tf_op jit(solution)/shard_map/ppermute | solution.py:13
  147.4 14.3 %collective-permute-start.5 = (bf16[4,128,768]{2,1,0:T(8,128)(2,1)}, bf16[4,128,768]{2,1,0:T(8,128)(2,1)}, u32[]{:S(2)}, u32[]{:S(2)}) collective-permute-start(bf16[4,128,768]{2,1,0:T(8,128)(2,1)} %collective-permute-done.4), channel_id=1, source_target_pairs={{0,1},{1,2},{2,3},{3,4},{4,5},{5,6},{6,7},{8,9},{9,10},{10,11},{11... | collective-permute-start | bytes 2359304 | tf_op jit(solution)/shard_map/ppermute | solution.py:13
  161.7 14.1 %collective-permute-start.6 = (bf16[4,128,768]{2,1,0:T(8,128)(2,1)}, bf16[4,128,768]{2,1,0:T(8,128)(2,1)S(1)}, u32[]{:S(2)}, u32[]{:S(2)}) collective-permute-start(bf16[4,128,768]{2,1,0:T(8,128)(2,1)} %collective-permute-done.5), channel_id=1, source_target_pairs={{0,1},{1,2},{2,3},{3,4},{4,5},{5,6},{6,7},{8,9},{9,10},{10,11},{11... | collective-permute-start | bytes 2359304 | tf_op jit(solution)/shard_map/ppermute | solution.py:13
  163.0 14.3 %copy-start.7 = (f32[128]{0:T(128)S(1)}, f32[128]{0:T(128)}, u32[]{:S(2)}) copy-start(f32[128]{0:T(128)} %param.14) | copy-start | bytes 1540
  175.8 13.3 %collective-permute-start.7 = (bf16[4,128,768]{2,1,0:T(8,128)(2,1)S(1)}, bf16[4,128,768]{2,1,0:T(8,128)(2,1)S(1)}, u32[]{:S(2)}, u32[]{:S(2)}) collective-permute-start(bf16[4,128,768]{2,1,0:T(8,128)(2,1)S(1)} %collective-permute-done.6), channel_id=1, source_target_pairs={{0,1},{1,2},{2,3},{3,4},{4,5},{5,6},{6,7},{8,9},{9,10},{10,11},{11... | collective-permute-start | bytes 2359304 | tf_op jit(solution)/shard_map/ppermute | solution.py:13
  177.8 13.8 %copy-start.3 = (bf16[4,128,768]{2,1,0:T(8,128)(2,1)S(1)}, bf16[4,128,768]{2,1,0:T(8,128)(2,1)}, u32[]{:S(2)}) copy-start(bf16[4,128,768]{2,1,0:T(8,128)(2,1)} %copy-done.2) | copy-start | bytes 2359300
  204.3 10.7 %copy-start.1 = (bf16[4,1152,384]{1,2,0:T(8,128)(2,1)S(1)}, bf16[4,1152,384]{1,2,0:T(8,128)(2,1)}, u32[]{:S(2)}) copy-start(bf16[4,1152,384]{1,2,0:T(8,128)(2,1)} %copy.29) | copy-start | bytes 10616836
  204.3 10.7 %copy-start.4 = (pred[128,1152]{0,1:T(8,128)(4,1)S(1)}, pred[128,1152]{0,1:T(8,128)(4,1)}, u32[]{:S(2)}) copy-start(pred[128,1152]{0,1:T(8,128)(4,1)} %fusion.19) | copy-start | bytes 442372
  204.3 19.4 %slice-start = ((s8[8257536]{0:T(1024)(128)(4,1)}), s8[4194304]{0:T(1024)(128)(4,1)S(1)}, s32[]{:S(2)}) async-start(s8[8257536]{0:T(1024)(128)(4,1)} %bitcast.70), calls=%async_computation.3 | async-start | bytes 8388608
  215.0 8.7 %slice-start.1 = ((s8[8257536]{0:T(1024)(128)(4,1)}), s8[4063232]{0:T(1024)(128)(4,1)S(1)}, s32[]{:S(2)}) async-start(s8[8257536]{0:T(1024)(128)(4,1)} %bitcast.70), calls=%async_computation.4 | async-start | bytes 8126464
  230.3 74.1 %copy-start = (bf16[1,128,5376]{2,1,0:T(8,128)(2,1)S(1)}, bf16[1,128,5376]{2,1,0:T(8,128)(2,1)}, u32[]{:S(2)}) copy-start(bf16[1,128,5376]{2,1,0:T(8,128)(2,1)} %param.9) | copy-start | bytes 4128772
  230.3 74.1 %copy-start.5 = (f32[5376]{0:T(1024)S(1)}, f32[5376]{0:T(1024)}, u32[]{:S(2)}) copy-start(f32[5376]{0:T(1024)} %param.17) | copy-start | bytes 64516
Sparse Core Ops, SparseCore 0:
  11.2 64.2 all-gather.1
  230.4 72.2 reduce-scatter.3
where the time goes:
time: 317 us; the launch traced here: 314 us
  waiting for transfers between devices  197 us (62%)
  matrix products  46.4 us (15%)
  local copies, waits for them, and re-layouts  34 us (11%)
  between operations  13.8 us (4%)
  other arithmetic  12.8 us (4%)
  starting transfers between devices  10.5 us (3%)
    unnamed x3, waiting for transfers between devices  72.4 us
    ppermute x8, waiting for transfers between devices, passed_along(): return lax.ppermute(shard, axis, pairs)  66.5 us
    all_gather x1, waiting for transfers between devices, per_device(): shard_rows = lax.all_gather(normalized_rows, 'fsdp', axis=0, tiled=True)  57.8 us
    unnamed x30, local copies, waits for them, and re-layouts  21.5 us
    dot_general x1, matrix products, per_device(): jnp.einsum('dqhgc,dkhc->dhgqk', query_rows, key_portion, preferred_elemen...  10.7 us
    ppermute x8, starting transfers between devices, passed_along(): return lax.ppermute(shard, axis, pairs)  10.4 us
    dot_general x1, matrix products, per_device(): jnp.einsum('dhgqk,dkhc->dqhgc', weights, value_portion, preferred_element...  8.7 us
    slice x2, local copies, waits for them, and re-layouts, per_device(): windowed[..., :kv_heads * head_dim]  8.33 us
  transfers between devices with their start and end apart: 10, of which 9 were waited for; matrix products, arithmetic and copies ran while one was open for 9% of the time, Pallas kernels for 0%

commit v1 on v0

v1 whole, which is shorter than its diff:
```python
import functools
import math

import jax
import jax.numpy as jnp
from jax import lax
from jax.experimental import pallas as pl
from jax.experimental.pallas import tpu as pltpu
from jax.sharding import PartitionSpec as P

epsilon = 1e-06
score_scale = 168.0 ** (-0.5)
window = 1024
MESH = pl.DeviceIdType.MESH
halves_of = ((0, 0), (1, 2), (2, 1), (3, 3))


def column_step(total, limit):
    step = 128
    for count in range(1, limit // 128 + 1):
        if total % (count * 128) == 0:
            step = count * 128
    return step


def layer_kernel(
    n_ctx, reach, q_heads, kv_heads, head,
    tok_hbm, wq_hbm, wk_hbm, wv_hbm, wo_hbm, pre_ref, post_ref, qg_ref, kg_ref, cos_ref, sin_ref,
    out_ref,
    tok, w, wo, nb, raw, q, kv, att, pb, rx, ry, dg,
    load_sem, ag_s, ag_r, rs_s, rs_r, z_s, z_r, b_s, b_r,
):
    f = lax.axis_index("fsdp")
    c = lax.axis_index("ctx")
    rows, features = tok.shape
    half = rows // 2
    z = c // 2
    p = c % 2
    nz = n_ctx // 2
    x_to = {"fsdp": f + 1 - 2 * (f % 2)}
    y_to = {"fsdp": (f + 2) % 4}
    sib = {"ctx": c + 1 - 2 * p}
    nxt = {"ctx": lax.rem(c + 2, n_ctx)}
    prv = {"ctx": lax.rem(c + n_ctx - 2, n_ctx)}
    has_next = z + 1 < nz
    has_prev = z > 0
    qw, kw = q_heads * head, kv_heads * head
    group = q_heads // kv_heads

    def load(i, src, dst):
        return pltpu.make_async_copy(src, dst, load_sem.at[i])

    loads = [load(0, tok_hbm, tok)]
    cut = features // 2
    for j, (src, lo, wide) in enumerate(((wk_hbm, qw, kw), (wv_hbm, qw + kw, kw), (wq_hbm, 0, qw))):
        for part in range(2):
            rs = pl.ds(part * cut, cut)
            loads.append(load(1 + 2 * j + part, src.at[rs], w.at[rs, pl.ds(lo, wide)]))
    wo_load = load(7, wo_hbm, wo)
    for d in loads:
        d.start()
    wo_load.start()

    barrier = pltpu.get_barrier_semaphore()
    for to in (x_to, y_to, sib):
        pl.semaphore_signal(barrier, inc=1, device_id=to, device_id_type=MESH)

    @pl.when(has_next)
    def _():
        pl.semaphore_signal(barrier, inc=1, device_id=nxt, device_id_type=MESH)

    @pl.when(has_prev)
    def _():
        pl.semaphore_signal(barrier, inc=1, device_id=prv, device_id_type=MESH)

    loads[0].wait()

    def norm_rows(i, carry):
        at = pl.ds(pl.multiple_of(i * 16, 16), 16)
        v = tok[at, :].astype(jnp.float32)
        mean_sq = jnp.mean(v * v, axis=-1, keepdims=True)
        nb[0, at, :] = (v * lax.rsqrt(mean_sq + epsilon) * pre_ref[...]).astype(jnp.bfloat16)
        return carry

    lax.fori_loop(0, rows // 16, norm_rows, 0)
    pl.semaphore_wait(barrier, 3 + jnp.minimum(z, 1) + jnp.minimum(nz - 1 - z, 1))

    A, B = pl.ds(0, half), pl.ds(half, half)

    def remote(src, dst, s, r, to):
        return pltpu.make_async_remote_copy(
            src_ref=src, dst_ref=dst, send_sem=s, recv_sem=r, device_id=to, device_id_type=MESH
        )

    def ag(i):
        src, dst, to = (
            (nb.at[0, A], nb.at[1, A], x_to),
            (nb.at[0, B], nb.at[2, B], x_to),
            (nb.at[0, B], nb.at[1, B], y_to),
            (nb.at[0, A], nb.at[2, A], y_to),
            (nb.at[1, A], nb.at[3, A], y_to),
            (nb.at[1, B], nb.at[3, B], x_to),
        )[i]
        return remote(src, dst, ag_s.at[i], ag_r.at[i], to)

    for i in (0, 2, 1, 3):
        ag(i).start()

    def z_copy(u, dz):
        return remote(kv.at[u, dz, p], kv.at[u, dz + 1, p], z_s.at[u, dz], z_r.at[u, dz + 1], nxt)

    def b_copy(u, dz):
        return remote(kv.at[u, dz, p], kv.at[u, dz, p], b_s.at[u, dz], b_r.at[u, dz], sib)

    def kv_arrived(u, dz):
        return remote(kv.at[u, dz, p], kv.at[u, dz, p], z_s.at[u, dz], z_r.at[u, dz], prv)

    def kv_paired(u, dz):
        return remote(kv.at[u, dz, 1 - p], kv.at[u, dz, 1 - p], b_s.at[u, dz], b_r.at[u, dz], sib)

    def send_own(u):
        @pl.when(has_next)
        def _():
            z_copy(u, 0).start()

        @pl.when(p == 0)
        def _():
            b_copy(u, 0).start()

    def relay(u, dz):
        if dz > reach:
            return

        @pl.when(z >= dz)
        def _():
            kv_arrived(u, dz).wait_recv()
            if dz < reach:
                @pl.when(has_next)
                def _():
                    z_copy(u, dz).start()
            b_copy(u, dz).start()

    def wait_pairs(u):
        @pl.when(p == 1)
        def _():
            kv_paired(u, 0).wait_recv()

        for dz in range(1, reach + 1):
            @pl.when(z >= dz)
            def _():
                kv_paired(u, dz).wait_recv()

    n_step = column_step(qw + 2 * kw, 256)

    def project(u):
        def columns(j, carry):
            at = pl.ds(pl.multiple_of(j * n_step, n_step), n_step)
            raw[:, at] = jnp.dot(nb[u], w[:, at], preferred_element_type=jnp.float32)
            return carry

        lax.fori_loop(0, (qw + 2 * kw) // n_step, columns, 0)

        def rotated(col, gain):
            v = raw[:, col : col + head]
            mean_sq = jnp.mean(v * v, axis=-1, keepdims=True)
            v = v * lax.rsqrt(mean_sq + epsilon) * gain[...]
            return (v * cos_ref[...] + pltpu.roll(v, head // 2, 1) * sin_ref[...]).astype(jnp.bfloat16)

        for h in range(kv_heads):
            kv[u, 0, p, :, h * head : (h + 1) * head] = rotated(qw + h * head, kg_ref)
        kv[u, 0, p, :, kw:] = raw[:, qw + kw :].astype(jnp.bfloat16)
        send_own(u)
        for h in range(q_heads):
            q[u, :, h * head : (h + 1) * head] = rotated(h * head, qg_ref)

    def attend(r):
        ua, ub = halves_of[r]

        def merged(first, second):
            return jnp.concatenate([first, second], axis=0)

        for g in range(kv_heads):
            kc = slice(g * head, (g + 1) * head)
            vc = slice(kw + g * head, kw + (g + 1) * head)

            def block(dz, par, cols):
                if ua == ub:
                    return kv[ua, dz, par, :, cols]
                return merged(kv[ua, dz, par, :half, cols], kv[ub, dz, par, half:, cols])

            parts = []
            for h in range(g * group, (g + 1) * group):
                hc = slice(h * head, (h + 1) * head)
                parts += [q[ua, :half, hc], q[ub, half:, hc]]
            qs = jnp.concatenate(parts, axis=0)

            def expo_of(keys):
                s = lax.dot_general(qs, keys, (((1,), (1,)), ((), ())), preferred_element_type=jnp.float32)
                return jnp.exp(s * score_scale)

            def times(e, values):
                return jnp.dot(e.astype(jnp.bfloat16), values, preferred_element_type=jnp.float32)

            qi = lax.broadcasted_iota(jnp.int32, (group, rows, rows), 1).reshape(group * rows, rows)
            kj = lax.broadcasted_iota(jnp.int32, (group * rows, rows), 1)
            e = jnp.where(kj <= qi, expo_of(block(0, p, kc)), 0.0)
            total, acc = e, times(e, block(0, p, vc))

            def beside(_, carry):
                total, acc = carry
                e = expo_of(block(0, 0, kc))
                return total + e, acc + times(e, block(0, 0, vc))

            def earlier(dz, carry):
                total, acc = carry
                e = expo_of(merged(block(dz, 0, kc), block(dz, 1, kc)))
                if n_ctx * rows > window:
                    apart = (p + 2 * dz) * rows + qi - kj
                    e = jnp.where(jnp.concatenate([apart, apart - rows], axis=1) < window, e, 0.0)
                acc = acc + times(e, merged(block(dz, 0, vc), block(dz, 1, vc)))
                return total + e[:, :rows] + e[:, rows:], acc

            total, acc = lax.fori_loop(0, p, beside, (total, acc))
            total, acc = lax.fori_loop(1, jnp.minimum(z, reach) + 1, earlier, (total, acc))
            o = (acc / jnp.sum(total, axis=-1, keepdims=True)).astype(jnp.bfloat16)
            for i in range(group):
                h = g * group + i
                hc = slice(h * head, (h + 1) * head)
                att[ua, :half, hc] = o[i * rows : i * rows + half]
                att[ub, half:, hc] = o[i * rows + half : (i + 1) * rows]

    o_step = column_step(features, 768)

    def output(u):
        def columns(j, carry):
            at = pl.ds(pl.multiple_of(j * o_step, o_step), o_step)
            pb[u, :, at] = jnp.dot(att[u], wo[:, at], preferred_element_type=jnp.float32).astype(jnp.bfloat16)
            return carry

        lax.fori_loop(0, features // o_step, columns, 0)

    quarter = half // 2
    A0, A1 = pl.ds(0, quarter), pl.ds(quarter, quarter)
    B0, B1 = pl.ds(half, quarter), pl.ds(half + quarter, quarter)

    def rs(i):
        src, dst, to = (
            (pb.at[1, A], rx.at[A], x_to),
            (pb.at[1, B], ry.at[B], y_to),
            (pb.at[3, A0], dg.at[A0], x_to),
            (pb.at[3, B0], dg.at[B0], y_to),
            (pb.at[3, A1], dg.at[A1], x_to),
            (pb.at[3, B1], dg.at[B1], y_to),
            (pb.at[2, A0], ry.at[A0], y_to),
            (pb.at[2, B0], rx.at[B0], x_to),
            (pb.at[2, A1], ry.at[A1], y_to),
            (pb.at[2, B1], rx.at[B1], x_to),
        )[i]
        return remote(src, dst, rs_s.at[i], rs_r.at[i], to)

    for d in loads[1:]:
        d.wait()
    project(0)
    ag(0).wait_recv()
    ag(4).start()
    ag(2).wait_recv()
    ag(5).start()
    relay(0, 1)
    project(1)
    relay(0, 2)
    relay(0, 3)
    relay(0, 4)
    relay(1, 1)
    wait_pairs(0)
    attend(0)
    wo_load.wait()
    output(0)
    relay(1, 2)
    ag(1).wait_recv()
    ag(3).wait_recv()
    project(2)
    relay(1, 3)
    relay(1, 4)
    relay(2, 1)
    ag(4).wait_recv()
    ag(5).wait_recv()
    project(3)
    relay(2, 2)
    relay(2, 3)
    relay(2, 4)
    relay(3, 1)
    wait_pairs(1)
    wait_pairs(2)
    attend(1)
    relay(3, 2)
    attend(2)
    output(1)
    rs(0).start()
    rs(1).start()
    relay(3, 3)
    relay(3, 4)
    wait_pairs(3)
    attend(3)
    output(3)
    for i in (2, 3, 4, 5):
        rs(i).start()
    output(2)

    def add_rows(first, count):
        def body(i, carry):
            at = pl.ds(pl.multiple_of(first + i * 16, 16), 16)
            pb[2, at, :] = (pb[2, at, :].astype(jnp.float32) + dg[at, :].astype(jnp.float32)).astype(jnp.bfloat16)
            return carry

        lax.fori_loop(0, count // 16, body, 0)

    for i, first in ((2, 0), (3, half), (4, quarter), (5, half + quarter)):
        rs(i).wait_recv()
        add_rows(first, quarter)
        rs(i + 4).start()

    def finish(first, count):
        def body(i, carry):
            at = pl.ds(pl.multiple_of(first + i * 16, 16), 16)
            summed = pb[0, at, :].astype(jnp.float32) + rx[at, :].astype(jnp.float32) + ry[at, :].astype(jnp.float32)
            mean_sq = jnp.mean(summed * summed, axis=-1, keepdims=True)
            normed = summed * lax.rsqrt(mean_sq + epsilon) * post_ref[...]
            out_ref[at, :] = (tok[at, :].astype(jnp.float32) + normed).astype(jnp.bfloat16)
            return carry

        lax.fori_loop(0, count // 16, body, 0)

    rs(0).wait_recv()
    rs(1).wait_recv()
    for i, first in ((6, 0), (7, half), (8, quarter), (9, half + quarter)):
        rs(i).wait_recv()
        finish(first, quarter)

    for i in range(6):
        ag(i).wait_send()
    for i in range(10):
        rs(i).wait_send()
    for u in range(4):
        @pl.when(has_next)
        def _():
            z_copy(u, 0).wait_send()

        @pl.when(p == 0)
        def _():
            b_copy(u, 0).wait_send()

        for dz in range(1, reach + 1):
            @pl.when(z >= dz)
            def _():
                if dz < reach:
                    @pl.when(has_next)
                    def _():
                        z_copy(u, dz).wait_send()
                b_copy(u, dz).wait_send()


def per_device(
    n_ctx, tokens, pre_gain, w_query, key_weight, value_weight, query_norm_gain, key_gain, w_out, post_gain
):
    _, rows, features = tokens.shape
    head = query_norm_gain.shape[0]
    qw, kw = w_query.shape[1], key_weight.shape[1]
    reach = min(n_ctx // 2 - 1, -(-window // (2 * rows)))
    half_dim = head // 2
    positions = lax.axis_index("ctx") * rows + jnp.arange(rows, dtype=jnp.int32)
    frequencies = 10000.0 ** (-jnp.arange(half_dim, dtype=jnp.float32) / half_dim)
    angles = positions.astype(jnp.float32)[:, None] * frequencies[None, :]
    cosine, sine = jnp.cos(angles), jnp.sin(angles)
    cos_all = jnp.concatenate([cosine, cosine], axis=1)
    sin_all = jnp.concatenate([-sine, sine], axis=1)
    any_spec = pl.BlockSpec(memory_space=pl.ANY)
    vmem_spec = pl.BlockSpec(memory_space=pltpu.VMEM)
    bf16 = jnp.bfloat16
    dma = pltpu.SemaphoreType.DMA
    out = pl.pallas_call(
        functools.partial(layer_kernel, n_ctx, reach, qw // head, kw // head, head),
        out_shape=jax.ShapeDtypeStruct((rows, features), bf16),
        in_specs=[any_spec] * 5 + [vmem_spec] * 6,
        out_specs=vmem_spec,
        scratch_shapes=[
            pltpu.VMEM((rows, features), bf16),
            pltpu.VMEM((features, qw + 2 * kw), bf16),
            pltpu.VMEM((qw, features), bf16),
            pltpu.VMEM((4, rows, features), bf16),
            pltpu.VMEM((rows, qw + 2 * kw), jnp.float32),
            pltpu.VMEM((4, rows, qw), bf16),
            pltpu.VMEM((4, reach + 1, 2, rows, 2 * kw), bf16),
            pltpu.VMEM((4, rows, qw), bf16),
            pltpu.VMEM((4, rows, features), bf16),
            pltpu.VMEM((rows, features), bf16),
            pltpu.VMEM((rows, features), bf16),
            pltpu.VMEM((rows, features), bf16),
            dma((8,)), dma((6,)), dma((6,)), dma((10,)), dma((10,)),
            dma((4, reach + 1)), dma((4, reach + 1)), dma((4, reach + 1)), dma((4, reach + 1)),
        ],
        compiler_params=pltpu.CompilerParams(
            collective_id=0, has_side_effects=True, vmem_limit_bytes=66_000_000
        ),
    )(
        tokens[0], w_query, key_weight, value_weight, w_out,
        pre_gain[None], post_gain[None], query_norm_gain[None], key_gain[None], cos_all, sin_all,
    )
    return out[None]


def solution(mesh):
    return jax.shard_map(
        functools.partial(per_device, mesh.shape["ctx"]),
        mesh=mesh,
        in_specs=(
            P("fsdp", "ctx", None),
            P(),
            P(None, "fsdp"),
            P(None, "fsdp"),
            P(None, "fsdp"),
            P(),
            P(),
            P("fsdp", None),
            P(),
        ),
        out_specs=P("fsdp", "ctx", None),
        check_vma=False,
    )
```

time: 317 us -> 132 us (0.42)
  waiting for transfers between devices: 197 us -> 0 us
  Pallas kernels: 0 us -> 125 us
  matrix products: 46.4 us -> 0 us
  local copies, waits for them, and re-layouts: 34 us -> 5.21 us
  between operations: 13.8 us -> 0.02 us
  other arithmetic: 12.8 us -> 1.07 us
  starting transfers between devices: 10.5 us -> 0 us
    pallas_call x0 -> x1, Pallas kernels: none -> 125 us  [per_device(): pl.pallas_call(functools.partial(layer_kernel, n_ctx, reach, qw // head,...]
    unnamed x3 -> x0, waiting for transfers between devices: 72.4 us -> none
    ppermute x8 -> x0, waiting for transfers between devices: 66.5 us -> none  [passed_along(): return lax.ppermute(shard, axis, pairs)]
    all_gather x1 -> x0, waiting for transfers between devices: 57.8 us -> none  [per_device(): shard_rows = lax.all_gather(normalized_rows, 'fsdp', axis=0, tiled=True)]
    dot_general x6 -> x0, matrix products: 46.4 us -> none  [the longest x1 10.7 us: per_device(): jnp.einsum('dqhgc,dkhc->dhgqk', query_rows, key_portion, preferred_elemen...]
    unnamed x30 -> x1, local copies, waits for them, and re-layouts: 21.5 us -> 2.51 us
    slice x3 -> x0, local copies, waits for them, and re-layouts: 12.4 us -> none  [the longest x2 8.33 us: per_device(): windowed[..., :kv_heads * head_dim]]
    ppermute x8 -> x0, starting transfers between devices: 10.4 us -> none  [passed_along(): return lax.ppermute(shard, axis, pairs)]
  transfers between devices with their start and end apart: 10 -> 0, of which waited for: 9 -> 0; matrix products, arithmetic and copies ran while one was open for 9% -> 0% of each run, Pallas kernels for 0% -> 0%
where the time goes in v1:
time: 132 us
  Pallas kernels  125 us (95%)
  local copies, waits for them, and re-layouts  5.21 us (4%)
    pallas_call x1, Pallas kernels, per_device(): pl.pallas_call(functools.partial(layer_kernel, n_ctx, reach, qw // head,...  125 us

profile of v1, /device:TPU:25, one launch (start us, length us, event | category | flops | bytes accessed | tf_op | source)
XLA Modules:
  0.0 131.5 jit_solution(13473334165679628982)
XLA Ops:
  0.0 1.4 %broadcast_in_dim.17.pre_ref = f32[1,5376]{1,0:T(1,128)} reshape(f32[5376]{0:T(1024)} %param.10) | data formatting | bytes 43008 | tf_op jit(solution)/shard_map/broadcast_in_dim | solution.py:406
  1.4 1.4 %broadcast_in_dim.18.post_ref = f32[1,5376]{1,0:T(1,128)} reshape(f32[5376]{0:T(1024)} %param.17) | data formatting | bytes 43008 | tf_op jit(solution)/shard_map/broadcast_in_dim | solution.py:406
  2.7 0.3 fusion
  3.0 0.7 pad_maximum_fusion
  3.8 125.2 %shard_map.91 = bf16[128,5376]{1,0:T(8,128)(2,1)} custom-call(bf16[128,5376]{1,0:T(8,128)(2,1)} %bitcast.5, bf16[5376,768]{1,0:T(8,128)(2,1)} %wq_hbm.1, bf16[5376,384]{1,0:T(8,128)(2,1)} %wk_hbm.1, bf16[5376,384]{1,0:T(8,128)(2,1)} %wv_hbm.1, bf16[768,5376]{1,0:T(8,128)(2,1)} %wo_hbm.1, f32[1,5376]{1,0:T(1,128)} %broadcast_in_dim.17.pre_ref, ...), custom_call_target="tpu_custom_call" | custom-call | tf_op jit(solution)/shard_map/pallas_call | solution.py:380
  129.0 2.5 %copy.11 = bf16[1,128,5376]{2,1,0:T(8,128)(2,1)} copy(bf16[1,128,5376]{2,1,0:T(8,128)(2,1)} %bitcast.4) | data formatting | bytes 2752512
  (2 shorter events, 0.0 us)

commit v2 on v1

--- a/solution.py
+++ b/solution.py
@@ -27,7 +27,7 @@
     n_ctx, reach, q_heads, kv_heads, head,
     tok_hbm, wq_hbm, wk_hbm, wv_hbm, wo_hbm, pre_ref, post_ref, qg_ref, kg_ref, cos_ref, sin_ref,
     out_ref,
-    tok, w, wo, nb, raw, q, kv, att, pb, rx, ry, dg,
+    tok, w, wo, nb, raw, q, kv, att, pb, rx, ry, dg, pre, post, accs, sums,
     load_sem, ag_s, ag_r, rs_s, rs_r, z_s, z_r, b_s, b_r,
 ):
     f = lax.axis_index("fsdp")
@@ -40,10 +40,14 @@
     x_to = {"fsdp": f + 1 - 2 * (f % 2)}
     y_to = {"fsdp": (f + 2) % 4}
     sib = {"ctx": c + 1 - 2 * p}
-    nxt = {"ctx": lax.rem(c + 2, n_ctx)}
-    prv = {"ctx": lax.rem(c + n_ctx - 2, n_ctx)}
-    has_next = z + 1 < nz
-    has_prev = z > 0
+
+    def ahead(step):
+        return {"ctx": lax.rem(c + 2 * step, n_ctx)}, z + step < nz
+
+    def behind(step):
+        return {"ctx": lax.rem(c + n_ctx - 2 * step, n_ctx)}, z >= step
+
+    direct = [step for step in (1, 3) if step <= reach]
     qw, kw = q_heads * head, kv_heads * head
     group = q_heads // kv_heads
 
@@ -65,25 +69,27 @@
     for to in (x_to, y_to, sib):
         pl.semaphore_signal(barrier, inc=1, device_id=to, device_id_type=MESH)
 
-    @pl.when(has_next)
-    def _():
-        pl.semaphore_signal(barrier, inc=1, device_id=nxt, device_id_type=MESH)
-
-    @pl.when(has_prev)
-    def _():
-        pl.semaphore_signal(barrier, inc=1, device_id=prv, device_id_type=MESH)
-
+    peers = 3
+    for step in direct:
+        for to, there in (ahead(step), behind(step)):
+            pl.when(there)(functools.partial(
+                pl.semaphore_signal, barrier, inc=1, device_id=to, device_id_type=MESH
+            ))
+        peers = peers + jnp.clip(z - step + 1, 0, 1) + jnp.clip(nz - z - step, 0, 1)
+
+    for wide, gain in ((pre, pre_ref), (post, post_ref)):
+        wide[...] = jnp.concatenate([gain[k : k + 1, :] for k in range(gain.shape[0])], axis=1)
     loads[0].wait()
 
     def norm_rows(i, carry):
         at = pl.ds(pl.multiple_of(i * 16, 16), 16)
         v = tok[at, :].astype(jnp.float32)
         mean_sq = jnp.mean(v * v, axis=-1, keepdims=True)
-        nb[0, at, :] = (v * lax.rsqrt(mean_sq + epsilon) * pre_ref[...]).astype(jnp.bfloat16)
+        nb[0, at, :] = (v * lax.rsqrt(mean_sq + epsilon) * pre[...]).astype(jnp.bfloat16)
         return carry
 
-    lax.fori_loop(0, rows // 16, norm_rows, 0)
-    pl.semaphore_wait(barrier, 3 + jnp.minimum(z, 1) + jnp.minimum(nz - 1 - z, 1))
+    lax.fori_loop(0, half // 16, norm_rows, 0)
+    pl.semaphore_wait(barrier, peers)
 
     A, B = pl.ds(0, half), pl.ds(half, half)
 
@@ -103,29 +109,45 @@
         )[i]
         return remote(src, dst, ag_s.at[i], ag_r.at[i], to)
 
-    for i in (0, 2, 1, 3):
+    ag(0).start()
+    lax.fori_loop(half // 16, rows // 16, norm_rows, 0)
+    for i in (2, 1, 3):
         ag(i).start()
 
-    def z_copy(u, dz):
-        return remote(kv.at[u, dz, p], kv.at[u, dz + 1, p], z_s.at[u, dz], z_r.at[u, dz + 1], nxt)
+    def z_copy(u, dz, step):
+        return remote(
+            kv.at[u, dz, p], kv.at[u, dz + step, p], z_s.at[u, dz + step], z_r.at[u, dz + step], ahead(step)[0]
+        )
 
     def b_copy(u, dz):
         return remote(kv.at[u, dz, p], kv.at[u, dz, p], b_s.at[u, dz], b_r.at[u, dz], sib)
 
     def kv_arrived(u, dz):
-        return remote(kv.at[u, dz, p], kv.at[u, dz, p], z_s.at[u, dz], z_r.at[u, dz], prv)
+        return remote(kv.at[u, dz, p], kv.at[u, dz, p], z_s.at[u, dz], z_r.at[u, dz], behind(1)[0])
 
     def kv_paired(u, dz):
         return remote(kv.at[u, dz, 1 - p], kv.at[u, dz, 1 - p], b_s.at[u, dz], b_r.at[u, dz], sib)
 
-    def send_own(u):
-        @pl.when(has_next)
-        def _():
-            z_copy(u, 0).start()
+    def own_copies(u, act):
+        for step in direct:
+            @pl.when(ahead(step)[1])
+            def _():
+                act(z_copy(u, 0, step))
 
         @pl.when(p == 0)
         def _():
-            b_copy(u, 0).start()
+            act(b_copy(u, 0))
+
+    def send_own(u):
+        own_copies(u, lambda d: d.start())
+
+    def passed_copies(u, dz, act):
+        if dz in direct and dz + 1 <= reach:
+            @pl.when(ahead(1)[1])
+            def _():
+                act(z_copy(u, dz, 1))
+
+        act(b_copy(u, dz))
 
     def relay(u, dz):
         if dz > reach:
@@ -134,11 +156,7 @@
         @pl.when(z >= dz)
         def _():
             kv_arrived(u, dz).wait_recv()
-            if dz < reach:
-                @pl.when(has_next)
-                def _():
-                    z_copy(u, dz).start()
-            b_copy(u, dz).start()
+            passed_copies(u, dz, lambda d: d.start())
 
     def wait_pairs(u):
         @pl.when(p == 1)
@@ -150,79 +168,90 @@
             def _():
                 kv_paired(u, dz).wait_recv()
 
-    n_step = column_step(qw + 2 * kw, 256)
-
-    def project(u):
+    k_step = column_step(2 * kw, 256)
+    q_step = column_step(qw, 256)
+
+    def columns_of(u, first, count, step):
         def columns(j, carry):
-            at = pl.ds(pl.multiple_of(j * n_step, n_step), n_step)
+            at = pl.ds(pl.multiple_of(first + j * step, 128), step)
             raw[:, at] = jnp.dot(nb[u], w[:, at], preferred_element_type=jnp.float32)
             return carry
 
-        lax.fori_loop(0, (qw + 2 * kw) // n_step, columns, 0)
-
-        def rotated(col, gain):
-            v = raw[:, col : col + head]
-            mean_sq = jnp.mean(v * v, axis=-1, keepdims=True)
-            v = v * lax.rsqrt(mean_sq + epsilon) * gain[...]
-            return (v * cos_ref[...] + pltpu.roll(v, head // 2, 1) * sin_ref[...]).astype(jnp.bfloat16)
-
+        lax.fori_loop(0, count // step, columns, 0)
+
+    def rotated(col, gain):
+        v = raw[:, col : col + head]
+        mean_sq = jnp.mean(v * v, axis=-1, keepdims=True)
+        v = v * lax.rsqrt(mean_sq + epsilon) * gain[...]
+        return (v * cos_ref[...] + pltpu.roll(v, head // 2, 1) * sin_ref[...]).astype(jnp.bfloat16)
+
+    def project_keys(u):
+        columns_of(u, qw, 2 * kw, k_step)
         for h in range(kv_heads):
             kv[u, 0, p, :, h * head : (h + 1) * head] = rotated(qw + h * head, kg_ref)
         kv[u, 0, p, :, kw:] = raw[:, qw + kw :].astype(jnp.bfloat16)
-        send_own(u)
+
+    def project_queries(u):
+        columns_of(u, 0, qw, q_step)
         for h in range(q_heads):
             q[u, :, h * head : (h + 1) * head] = rotated(h * head, qg_ref)
 
-    def attend(r):
-        ua, ub = halves_of[r]
-
-        def merged(first, second):
-            return jnp.concatenate([first, second], axis=0)
-
-        for g in range(kv_heads):
-            kc = slice(g * head, (g + 1) * head)
-            vc = slice(kw + g * head, kw + (g + 1) * head)
-
-            def block(dz, par, cols):
-                if ua == ub:
-                    return kv[ua, dz, par, :, cols]
-                return merged(kv[ua, dz, par, :half, cols], kv[ub, dz, par, half:, cols])
-
-            parts = []
-            for h in range(g * group, (g + 1) * group):
-                hc = slice(h * head, (h + 1) * head)
-                parts += [q[ua, :half, hc], q[ub, half:, hc]]
-            qs = jnp.concatenate(parts, axis=0)
-
-            def expo_of(keys):
-                s = lax.dot_general(qs, keys, (((1,), (1,)), ((), ())), preferred_element_type=jnp.float32)
-                return jnp.exp(s * score_scale)
-
-            def times(e, values):
-                return jnp.dot(e.astype(jnp.bfloat16), values, preferred_element_type=jnp.float32)
-
-            qi = lax.broadcasted_iota(jnp.int32, (group, rows, rows), 1).reshape(group * rows, rows)
-            kj = lax.broadcasted_iota(jnp.int32, (group * rows, rows), 1)
-            e = jnp.where(kj <= qi, expo_of(block(0, p, kc)), 0.0)
-            total, acc = e, times(e, block(0, p, vc))
-
-            def beside(_, carry):
-                total, acc = carry
-                e = expo_of(block(0, 0, kc))
-                return total + e, acc + times(e, block(0, 0, vc))
-
-            def earlier(dz, carry):
-                total, acc = carry
-                e = expo_of(merged(block(dz, 0, kc), block(dz, 1, kc)))
-                if n_ctx * rows > window:
-                    apart = (p + 2 * dz) * rows + qi - kj
-                    e = jnp.where(jnp.concatenate([apart, apart - rows], axis=1) < window, e, 0.0)
-                acc = acc + times(e, merged(block(dz, 0, vc), block(dz, 1, vc)))
-                return total + e[:, :rows] + e[:, rows:], acc
-
-            total, acc = lax.fori_loop(0, p, beside, (total, acc))
-            total, acc = lax.fori_loop(1, jnp.minimum(z, reach) + 1, earlier, (total, acc))
-            o = (acc / jnp.sum(total, axis=-1, keepdims=True)).astype(jnp.bfloat16)
+    def merged(parts):
+        return jnp.concatenate(parts, axis=0)
+
+    def attend(docs):
+        qi = lax.broadcasted_iota(jnp.int32, (group, rows, rows), 1).reshape(group * rows, rows)
+        kj = lax.broadcasted_iota(jnp.int32, (group * rows, rows), 1)
+        streams = [(i * kv_heads + g, g, halves_of[r]) for i, r in enumerate(docs) for g in range(kv_heads)]
+
+        def block(units, dz, par, cols):
+            ua, ub = units
+            if ua == ub:
+                return kv[ua, dz, par, :, cols]
+            return merged([kv[ua, dz, par, :half, cols], kv[ub, dz, par, half:, cols]])
+
+        def step(dz, pars, mask, first=False):
+            for n, g, (ua, ub) in streams:
+                kc = slice(g * head, (g + 1) * head)
+                vc = slice(kw + g * head, kw + (g + 1) * head)
+                parts = []
+                for h in range(g * group, (g + 1) * group):
+                    hc = slice(h * head, (h + 1) * head)
+                    parts += [q[ua, :half, hc], q[ub, half:, hc]]
+                keys = merged([block((ua, ub), dz, par, kc) for par in pars])
+                values = merged([block((ua, ub), dz, par, vc) for par in pars])
+                s = lax.dot_general(
+                    merged(parts), keys, (((1,), (1,)), ((), ())), preferred_element_type=jnp.float32
+                )
+                e = jnp.exp(s * score_scale)
+                if mask is not None:
+                    e = jnp.where(mask, e, 0.0)
+                total = sum(e[:, i * rows : (i + 1) * rows] for i in range(len(pars)))
+                acc = jnp.dot(e.astype(jnp.bfloat16), values, preferred_element_type=jnp.float32)
+                if first:
+                    sums[n], accs[n] = total, acc
+                else:
+                    sums[n] += total
+                    accs[n] += acc
+
+        step(0, [p], kj <= qi, True)
+
+        def beside(_, carry):
+            step(0, [0], None)
+            return carry
+
+        def earlier(dz, carry):
+            mask = None
+            if n_ctx * rows > window:
+                apart = (p + 2 * dz) * rows + qi - kj
+                mask = jnp.concatenate([apart, apart - rows], axis=1) < window
+            step(dz, [0, 1], mask)
+            return carry
+
+        lax.fori_loop(0, p, beside, 0)
+        lax.fori_loop(1, jnp.minimum(z, reach) + 1, earlier, 0)
+        for n, g, (ua, ub) in streams:
+            o = (accs[n] / jnp.sum(sums[n], axis=-1, keepdims=True)).astype(jnp.bfloat16)
             for i in range(group):
                 h = g * group + i
                 hc = slice(h * head, (h + 1) * head)
@@ -260,51 +289,54 @@
 
     for d in loads[1:]:
         d.wait()
-    project(0)
+    project_keys(0)
     ag(0).wait_recv()
     ag(4).start()
     ag(2).wait_recv()
     ag(5).start()
-    relay(0, 1)
-    project(1)
-    relay(0, 2)
-    relay(0, 3)
-    relay(0, 4)
+    project_keys(1)
+    send_own(1)
+    project_queries(1)
     relay(1, 1)
-    wait_pairs(0)
-    attend(0)
-    wo_load.wait()
-    output(0)
-    relay(1, 2)
+    project_queries(0)
     ag(1).wait_recv()
     ag(3).wait_recv()
-    project(2)
-    relay(1, 3)
-    relay(1, 4)
+    project_keys(2)
+    send_own(2)
+    for dz in range(2, reach + 1):
+        relay(1, dz)
+    project_queries(2)
     relay(2, 1)
     ag(4).wait_recv()
     ag(5).wait_recv()
-    project(3)
-    relay(2, 2)
-    relay(2, 3)
-    relay(2, 4)
-    relay(3, 1)
+    project_keys(3)
+    send_own(3)
+    send_own(0)
+    for dz in range(2, reach + 1):
+        relay(2, dz)
+    wo_load.wait()
     wait_pairs(1)
     wait_pairs(2)
-    attend(1)
-    relay(3, 2)
-    attend(2)
+    attend((1, 2))
+    relay(3, 1)
     output(1)
     rs(0).start()
     rs(1).start()
-    relay(3, 3)
-    relay(3, 4)
+    project_queries(3)
+    relay(0, 1)
+    for dz in range(2, reach + 1):
+        relay(3, dz)
     wait_pairs(3)
-    attend(3)
+    attend((3,))
     output(3)
     for i in (2, 3, 4, 5):
         rs(i).start()
     output(2)
+    for dz in range(2, reach + 1):
+        relay(0, dz)
+    wait_pairs(0)
+    attend((0,))
+    output(0)
 
     def add_rows(first, count):
         def body(i, carry):
@@ -324,7 +356,7 @@
             at = pl.ds(pl.multiple_of(first + i * 16, 16), 16)
             summed = pb[0, at, :].astype(jnp.float32) + rx[at, :].astype(jnp.float32) + ry[at, :].astype(jnp.float32)
             mean_sq = jnp.mean(summed * summed, axis=-1, keepdims=True)
-            normed = summed * lax.rsqrt(mean_sq + epsilon) * post_ref[...]
+            normed = summed * lax.rsqrt(mean_sq + epsilon) * post[...]
             out_ref[at, :] = (tok[at, :].astype(jnp.float32) + normed).astype(jnp.bfloat16)
             return carry
 
@@ -341,22 +373,11 @@
     for i in range(10):
         rs(i).wait_send()
     for u in range(4):
-        @pl.when(has_next)
-        def _():
-            z_copy(u, 0).wait_send()
-
-        @pl.when(p == 0)
-        def _():
-            b_copy(u, 0).wait_send()
-
+        own_copies(u, lambda d: d.wait_send())
         for dz in range(1, reach + 1):
             @pl.when(z >= dz)
             def _():
-                if dz < reach:
-                    @pl.when(has_next)
-                    def _():
-                        z_copy(u, dz).wait_send()
-                b_copy(u, dz).wait_send()
+                passed_copies(u, dz, lambda d: d.wait_send())
 
 
 def per_device(
@@ -395,6 +416,10 @@
             pltpu.VMEM((rows, features), bf16),
             pltpu.VMEM((rows, features), bf16),
             pltpu.VMEM((rows, features), bf16),
+            pltpu.VMEM((1, features), jnp.float32),
+            pltpu.VMEM((1, features), jnp.float32),
+            pltpu.VMEM((2 * kw // head, qw // kw * rows, head), jnp.float32),
+            pltpu.VMEM((2 * kw // head, qw // kw * rows, rows), jnp.float32),
             dma((8,)), dma((6,)), dma((6,)), dma((10,)), dma((10,)),
             dma((4, reach + 1)), dma((4, reach + 1)), dma((4, reach + 1)), dma((4, reach + 1)),
         ],
@@ -403,7 +428,7 @@
         ),
     )(
         tokens[0], w_query, key_weight, value_weight, w_out,
-        pre_gain[None], post_gain[None], query_norm_gain[None], key_gain[None], cos_all, sin_all,
+        pre_gain.reshape(-1, 128), post_gain.reshape(-1, 128), query_norm_gain[None], key_gain[None], cos_all, sin_all,
     )
     return out[None]
 

time: 132 us -> 119 us (0.902)
  Pallas kernels: 125 us -> 115 us
  local copies, waits for them, and re-layouts: 5.21 us -> 2.51 us
    pallas_call x1, Pallas kernels: 125 us -> 115 us  [per_device(): pl.pallas_call(functools.partial(layer_kernel, n_ctx, reach, qw // head,...]
    broadcast_in_dim x2 -> x0, local copies, waits for them, and re-layouts: 2.7 us -> none  [the longest x1 1.35 us: per_device(): pre_gain[None]]
where the time goes in v2:
time: 119 us; the launch traced here: 118 us
  Pallas kernels  115 us (97%)
  local copies, waits for them, and re-layouts  2.51 us (2%)
    pallas_call x1, Pallas kernels, per_device(): pl.pallas_call(functools.partial(layer_kernel, n_ctx, reach, qw // head,...  115 us
    unnamed x1, local copies, waits for them, and re-layouts  2.51 us

profile of v2, /device:TPU:25, one launch (start us, length us, event | category | flops | bytes accessed | tf_op | source)
XLA Modules:
  0.0 118.4 jit_solution(1075965455285511762)
XLA Ops:
  0.0 0.3 fusion
  0.3 0.7 pad_maximum_fusion
  1.1 114.8 %shard_map.91 = bf16[128,5376]{1,0:T(8,128)(2,1)} custom-call(bf16[128,5376]{1,0:T(8,128)(2,1)} %bitcast.7, bf16[5376,768]{1,0:T(8,128)(2,1)} %wq_hbm.1, bf16[5376,384]{1,0:T(8,128)(2,1)} %wk_hbm.1, bf16[5376,384]{1,0:T(8,128)(2,1)} %wv_hbm.1, bf16[768,5376]{1,0:T(8,128)(2,1)} %wo_hbm.1, f32[42,128]{1,0:T(8,128)} %bitcast.8, f32[42,128]{1,0:T(8,128)} %bitcast.9, ...), custom_call_target="tpu_custom_call" | custom-call | tf_op jit(solution)/shard_map/pallas_call | solution.py:401
  115.9 2.5 %copy.11 = bf16[1,128,5376]{2,1,0:T(8,128)(2,1)} copy(bf16[1,128,5376]{2,1,0:T(8,128)(2,1)} %bitcast.6) | data formatting | bytes 2752512
  (2 shorter events, 0.0 us)

commit v3 on v2

--- a/solution.py
+++ b/solution.py
@@ -11,6 +11,7 @@
 epsilon = 1e-06
 score_scale = 168.0 ** (-0.5)
 window = 1024
+vmem_limit = 58_000_000
 MESH = pl.DeviceIdType.MESH
 halves_of = ((0, 0), (1, 2), (2, 1), (3, 3))
 
@@ -54,16 +55,16 @@
     def load(i, src, dst):
         return pltpu.make_async_copy(src, dst, load_sem.at[i])
 
-    loads = [load(0, tok_hbm, tok)]
+    tok_loads = [load(i, tok_hbm.at[pl.ds(i * half, half)], tok.at[pl.ds(i * half, half)]) for i in range(2)]
+    for d in tok_loads:
+        d.start()
+    loads = []
     cut = features // 2
     for j, (src, lo, wide) in enumerate(((wk_hbm, qw, kw), (wv_hbm, qw + kw, kw), (wq_hbm, 0, qw))):
         for part in range(2):
             rs = pl.ds(part * cut, cut)
-            loads.append(load(1 + 2 * j + part, src.at[rs], w.at[rs, pl.ds(lo, wide)]))
-    wo_load = load(7, wo_hbm, wo)
-    for d in loads:
-        d.start()
-    wo_load.start()
+            loads.append(load(2 + 2 * j + part, src.at[rs], w.at[rs, pl.ds(lo, wide)]))
+    wo_load = load(8, wo_hbm, wo)
 
     barrier = pltpu.get_barrier_semaphore()
     for to in (x_to, y_to, sib):
@@ -79,7 +80,7 @@
 
     for wide, gain in ((pre, pre_ref), (post, post_ref)):
         wide[...] = jnp.concatenate([gain[k : k + 1, :] for k in range(gain.shape[0])], axis=1)
-    loads[0].wait()
+    tok_loads[0].wait()
 
     def norm_rows(i, carry):
         at = pl.ds(pl.multiple_of(i * 16, 16), 16)
@@ -89,6 +90,10 @@
         return carry
 
     lax.fori_loop(0, half // 16, norm_rows, 0)
+    tok_loads[1].wait()
+    for d in loads:
+        d.start()
+    wo_load.start()
     pl.semaphore_wait(barrier, peers)
 
     A, B = pl.ds(0, half), pl.ds(half, half)
@@ -199,10 +204,17 @@
     def merged(parts):
         return jnp.concatenate(parts, axis=0)
 
-    def attend(docs):
-        qi = lax.broadcasted_iota(jnp.int32, (group, rows, rows), 1).reshape(group * rows, rows)
-        kj = lax.broadcasted_iota(jnp.int32, (group * rows, rows), 1)
-        streams = [(i * kv_heads + g, g, halves_of[r]) for i, r in enumerate(docs) for g in range(kv_heads)]
+    def attend(u):
+        own, other = halves_of[u], halves_of[(0, 2, 1, 3)[u]]
+        spans = [(0, rows, own)] if own == other else [(0, half, own), (half, half, other)]
+        streams = [
+            (i * kv_heads + g, g, lo, size, units)
+            for i, (lo, size, units) in enumerate(spans) for g in range(kv_heads)
+        ]
+
+        def places(lo, size):
+            qi = lax.broadcasted_iota(jnp.int32, (group, size, rows), 1).reshape(group * size, rows) + lo
+            return qi, lax.broadcasted_iota(jnp.int32, (group * size, rows), 1)
 
         def block(units, dz, par, cols):
             ua, ub = units
@@ -211,52 +223,54 @@
             return merged([kv[ua, dz, par, :half, cols], kv[ub, dz, par, half:, cols]])
 
         def step(dz, pars, mask, first=False):
-            for n, g, (ua, ub) in streams:
+            for n, g, lo, size, units in streams:
                 kc = slice(g * head, (g + 1) * head)
                 vc = slice(kw + g * head, kw + (g + 1) * head)
-                parts = []
-                for h in range(g * group, (g + 1) * group):
-                    hc = slice(h * head, (h + 1) * head)
-                    parts += [q[ua, :half, hc], q[ub, half:, hc]]
-                keys = merged([block((ua, ub), dz, par, kc) for par in pars])
-                values = merged([block((ua, ub), dz, par, vc) for par in pars])
-                s = lax.dot_general(
-                    merged(parts), keys, (((1,), (1,)), ((), ())), preferred_element_type=jnp.float32
-                )
+                at = slice(0, group * size)
+                queries = merged([
+                    q[u, lo : lo + size, h * head : (h + 1) * head] for h in range(g * group, (g + 1) * group)
+                ])
+                keys = merged([block(units, dz, par, kc) for par in pars])
+                values = merged([block(units, dz, par, vc) for par in pars])
+                s = lax.dot_general(queries, keys, (((1,), (1,)), ((), ())), preferred_element_type=jnp.float32)
                 e = jnp.exp(s * score_scale)
                 if mask is not None:
-                    e = jnp.where(mask, e, 0.0)
+                    e = jnp.where(mask(lo, size), e, 0.0)
                 total = sum(e[:, i * rows : (i + 1) * rows] for i in range(len(pars)))
                 acc = jnp.dot(e.astype(jnp.bfloat16), values, preferred_element_type=jnp.float32)
                 if first:
-                    sums[n], accs[n] = total, acc
+                    sums[n, at], accs[n, at] = total, acc
                 else:
-                    sums[n] += total
-                    accs[n] += acc
-
-        step(0, [p], kj <= qi, True)
+                    sums[n, at] += total
+                    accs[n, at] += acc
+
+        def causal(lo, size):
+            qi, kj = places(lo, size)
+            return kj <= qi
+
+        step(0, [p], causal, True)
 
         def beside(_, carry):
             step(0, [0], None)
             return carry
 
         def earlier(dz, carry):
-            mask = None
-            if n_ctx * rows > window:
+            def near(lo, size):
+                qi, kj = places(lo, size)
                 apart = (p + 2 * dz) * rows + qi - kj
-                mask = jnp.concatenate([apart, apart - rows], axis=1) < window
-            step(dz, [0, 1], mask)
+                return jnp.concatenate([apart, apart - rows], axis=1) < window
+
+            step(dz, [0, 1], near if n_ctx * rows > window else None)
             return carry
 
         lax.fori_loop(0, p, beside, 0)
         lax.fori_loop(1, jnp.minimum(z, reach) + 1, earlier, 0)
-        for n, g, (ua, ub) in streams:
-            o = (accs[n] / jnp.sum(sums[n], axis=-1, keepdims=True)).astype(jnp.bfloat16)
+        for n, g, lo, size, _ in streams:
+            at = slice(0, group * size)
+            o = (accs[n, at] / jnp.sum(sums[n, at], axis=-1, keepdims=True)).astype(jnp.bfloat16)
             for i in range(group):
                 h = g * group + i
-                hc = slice(h * head, (h + 1) * head)
-                att[ua, :half, hc] = o[i * rows : i * rows + half]
-                att[ub, half:, hc] = o[i * rows + half : (i + 1) * rows]
+                att[u, lo : lo + size, h * head : (h + 1) * head] = o[i * size : (i + 1) * size]
 
     o_step = column_step(features, 768)
 
@@ -287,7 +301,7 @@
         )[i]
         return remote(src, dst, rs_s.at[i], rs_r.at[i], to)
 
-    for d in loads[1:]:
+    for d in loads:
         d.wait()
     project_keys(0)
     ag(0).wait_recv()
@@ -317,26 +331,22 @@
     wo_load.wait()
     wait_pairs(1)
     wait_pairs(2)
-    attend((1, 2))
-    relay(3, 1)
+    attend(1)
     output(1)
     rs(0).start()
     rs(1).start()
+    relay(3, 1)
+    attend(2)
     project_queries(3)
     relay(0, 1)
     for dz in range(2, reach + 1):
         relay(3, dz)
     wait_pairs(3)
-    attend((3,))
+    attend(3)
     output(3)
     for i in (2, 3, 4, 5):
         rs(i).start()
     output(2)
-    for dz in range(2, reach + 1):
-        relay(0, dz)
-    wait_pairs(0)
-    attend((0,))
-    output(0)
 
     def add_rows(first, count):
         def body(i, carry):
@@ -350,6 +360,11 @@
         rs(i).wait_recv()
         add_rows(first, quarter)
         rs(i + 4).start()
+    for dz in range(2, reach + 1):
+        relay(0, dz)
+    wait_pairs(0)
+    attend(0)
+    output(0)
 
     def finish(first, count):
         def body(i, carry):
@@ -420,11 +435,11 @@
             pltpu.VMEM((1, features), jnp.float32),
             pltpu.VMEM((2 * kw // head, qw // kw * rows, head), jnp.float32),
             pltpu.VMEM((2 * kw // head, qw // kw * rows, rows), jnp.float32),
-            dma((8,)), dma((6,)), dma((6,)), dma((10,)), dma((10,)),
+            dma((9,)), dma((6,)), dma((6,)), dma((10,)), dma((10,)),
             dma((4, reach + 1)), dma((4, reach + 1)), dma((4, reach + 1)), dma((4, reach + 1)),
         ],
         compiler_params=pltpu.CompilerParams(
-            collective_id=0, has_side_effects=True, vmem_limit_bytes=66_000_000
+            collective_id=0, has_side_effects=True, vmem_limit_bytes=vmem_limit
         ),
     )(
         tokens[0], w_query, key_weight, value_weight, w_out,

time: 119 us -> 118 us (level)
  no operation moved by 1% of the time
where the time goes in v3:
time: 118 us
  Pallas kernels  115 us (97%)
  local copies, waits for them, and re-layouts  2.51 us (2%)
    pallas_call x1, Pallas kernels, per_device(): pl.pallas_call(functools.partial(layer_kernel, n_ctx, reach, qw // head,...  115 us
    unnamed x1, local copies, waits for them, and re-layouts  2.51 us

profile of v3, /device:TPU:25, one launch (start us, length us, event | category | flops | bytes accessed | tf_op | source)
XLA Modules:
  0.0 118.2 jit_solution(3494121294131392439)
XLA Ops:
  0.0 0.3 fusion
  0.3 0.7 pad_maximum_fusion
  1.1 114.6 %shard_map.91 = bf16[128,5376]{1,0:T(8,128)(2,1)} custom-call(bf16[128,5376]{1,0:T(8,128)(2,1)} %bitcast.7, bf16[5376,768]{1,0:T(8,128)(2,1)} %wq_hbm.1, bf16[5376,384]{1,0:T(8,128)(2,1)} %wk_hbm.1, bf16[5376,384]{1,0:T(8,128)(2,1)} %wv_hbm.1, bf16[768,5376]{1,0:T(8,128)(2,1)} %wo_hbm.1, f32[42,128]{1,0:T(8,128)} %bitcast.8, f32[42,128]{1,0:T(8,128)} %bitcast.9, ...), custom_call_target="tpu_custom_call" | custom-call | tf_op jit(solution)/shard_map/pallas_call | solution.py:416
  115.7 2.5 %copy.11 = bf16[1,128,5376]{2,1,0:T(8,128)(2,1)} copy(bf16[1,128,5376]{2,1,0:T(8,128)(2,1)} %bitcast.6) | data formatting | bytes 2752512
  (2 shorter events, 0.0 us)

commit v4 on v3

--- a/solution.py
+++ b/solution.py
@@ -325,7 +325,6 @@
     ag(5).wait_recv()
     project_keys(3)
     send_own(3)
-    send_own(0)
     for dz in range(2, reach + 1):
         relay(2, dz)
     wo_load.wait()
@@ -338,15 +337,16 @@
     relay(3, 1)
     attend(2)
     project_queries(3)
-    relay(0, 1)
     for dz in range(2, reach + 1):
         relay(3, dz)
+    send_own(0)
     wait_pairs(3)
     attend(3)
     output(3)
     for i in (2, 3, 4, 5):
         rs(i).start()
     output(2)
+    relay(0, 1)
 
     def add_rows(first, count):
         def body(i, carry):

time: 118 us -> 111 us (0.941)
  Pallas kernels: 115 us -> 107 us
    pallas_call x1, Pallas kernels: 115 us -> 107 us  [per_device(): pl.pallas_call(functools.partial(layer_kernel, n_ctx, reach, qw // head,...]
where the time goes in v4:
time: 111 us
  Pallas kernels  107 us (96%)
  local copies, waits for them, and re-layouts  2.51 us (2%)
    pallas_call x1, Pallas kernels, per_device(): pl.pallas_call(functools.partial(layer_kernel, n_ctx, reach, qw // head,...  107 us
    unnamed x1, local copies, waits for them, and re-layouts  2.51 us

profile of v4, /device:TPU:25, one launch (start us, length us, event | category | flops | bytes accessed | tf_op | source)
XLA Modules:
  0.0 110.9 jit_solution(7339485653361481783)
XLA Ops:
  0.0 0.3 fusion
  0.3 0.7 pad_maximum_fusion
  1.1 107.3 %shard_map.91 = bf16[128,5376]{1,0:T(8,128)(2,1)} custom-call(bf16[128,5376]{1,0:T(8,128)(2,1)} %bitcast.7, bf16[5376,768]{1,0:T(8,128)(2,1)} %wq_hbm.1, bf16[5376,384]{1,0:T(8,128)(2,1)} %wk_hbm.1, bf16[5376,384]{1,0:T(8,128)(2,1)} %wv_hbm.1, bf16[768,5376]{1,0:T(8,128)(2,1)} %wo_hbm.1, f32[42,128]{1,0:T(8,128)} %bitcast.8, f32[42,128]{1,0:T(8,128)} %bitcast.9, ...), custom_call_target="tpu_custom_call" | custom-call | tf_op jit(solution)/shard_map/pallas_call | solution.py:416
  108.4 2.5 %copy.11 = bf16[1,128,5376]{2,1,0:T(8,128)(2,1)} copy(bf16[1,128,5376]{2,1,0:T(8,128)(2,1)} %bitcast.6) | data formatting | bytes 2752512
  (2 shorter events, 0.0 us)

commit v5 on v4

--- a/solution.py
+++ b/solution.py
@@ -321,11 +321,12 @@
         relay(1, dz)
     project_queries(2)
     relay(2, 1)
+    relay(2, 2)
     ag(4).wait_recv()
     ag(5).wait_recv()
     project_keys(3)
     send_own(3)
-    for dz in range(2, reach + 1):
+    for dz in range(3, reach + 1):
         relay(2, dz)
     wo_load.wait()
     wait_pairs(1)

time: 111 us -> 111 us (level)
  no operation moved by 1% of the time
where the time goes in v5:
time: 111 us
  Pallas kernels  107 us (96%)
  local copies, waits for them, and re-layouts  2.51 us (2%)
    pallas_call x1, Pallas kernels, per_device(): pl.pallas_call(functools.partial(layer_kernel, n_ctx, reach, qw // head,...  107 us
    unnamed x1, local copies, waits for them, and re-layouts  2.51 us

profile of v5, /device:TPU:25, one launch (start us, length us, event | category | flops | bytes accessed | tf_op | source)
XLA Modules:
  0.0 110.7 jit_solution(84699237063086243)
XLA Ops:
  0.0 0.3 fusion
  0.3 0.7 pad_maximum_fusion
  1.1 107.1 %shard_map.91 = bf16[128,5376]{1,0:T(8,128)(2,1)} custom-call(bf16[128,5376]{1,0:T(8,128)(2,1)} %bitcast.7, bf16[5376,768]{1,0:T(8,128)(2,1)} %wq_hbm.1, bf16[5376,384]{1,0:T(8,128)(2,1)} %wk_hbm.1, bf16[5376,384]{1,0:T(8,128)(2,1)} %wv_hbm.1, bf16[768,5376]{1,0:T(8,128)(2,1)} %wo_hbm.1, f32[42,128]{1,0:T(8,128)} %bitcast.8, f32[42,128]{1,0:T(8,128)} %bitcast.9, ...), custom_call_target="tpu_custom_call" | custom-call | tf_op jit(solution)/shard_map/pallas_call | solution.py:417
  108.2 2.5 %copy.11 = bf16[1,128,5376]{2,1,0:T(8,128)(2,1)} copy(bf16[1,128,5376]{2,1,0:T(8,128)(2,1)} %bitcast.6) | data formatting | bytes 2752512
  (2 shorter events, 0.0 us)
